TPU v7x, 32 devices: a whole 2x2x4 slice. The times are simulated.
32 devices in a mesh: cuts: 2 (over y), group: 16 (over z, x, core).
Axes of the slice: x: 2, y: 2, z: 4, core: 2. Of those that a mesh axis runs over, the one named last changes fastest.
Arguments:
- stem_blocks: bfloat16 [2, 64, 1024, 512], P('cuts', None, 'group'), may hold values from -6 to 6
- cap_tensor: bfloat16 [2, 2, 256, 256], P('cuts'), may hold values from -0.1875 to 0.1875
- slot_rows: int32 [64, 1024], P('group'), may hold values from 0 to 1023
- counts: int32 [64], P('group'), may hold values from 128 to 1024, as said below
Outputs:
- amplitudes: bfloat16 [1024, 64, 512], P('cuts', 'group')
Inputs may be any that keep to these rules, and one draw needn't show every extreme that they name: `counts`: some group has exactly 1024 live slots in every draw.
All inputs are finite; a program needn't handle non-finite values.
Results may differ from a plain program's by a relative error of at most 0.0052.
Values may be sent and summed in bfloat16 or wider, within the bound.
No kernel may reach another device: no remote copies, remote signals or barrier semaphores. Data moves between devices by JAX's collectives and lax.ppermute only.
A program may use at most 64 MiB of HBM per device.

v0:
```python
import jax
import jax.numpy as jnp
from jax import lax
from jax.sharding import PartitionSpec as P


def build_matrix(cap_pair):
    real_part = cap_pair[0]
    imag_part = cap_pair[1]
    upper = jnp.concatenate([real_part, imag_part], axis=1)
    lower = jnp.concatenate([-imag_part, real_part], axis=1)
    return jnp.concatenate([upper, lower], axis=0)


def local(stem_blocks, cap_tensor, slot_rows, counts):
    owned_rows = lax.all_to_all(stem_blocks[0], "group", split_axis=0, concat_axis=1, tiled=True)
    matrix = build_matrix(cap_tensor[0])
    slot_total = slot_rows.shape[1]
    share = slot_total // lax.axis_size("cuts")
    positions = jnp.arange(slot_total, dtype=jnp.int32)
    live_mask = positions[None, :] < counts[:, None]
    picked = jnp.take_along_axis(owned_rows, slot_rows[:, :, None], axis=1)
    product = jnp.einsum("gcr,rs->cgs", picked, matrix, preferred_element_type=jnp.float32)
    whole_sum = lax.psum(
        jnp.where(jnp.transpose(live_mask)[:, :, None], product, jnp.float32(0.0)).astype(
            jnp.bfloat16
        ),
        "cuts",
    ).astype(jnp.float32)
    summed = lax.dynamic_slice_in_dim(whole_sum, lax.axis_index("cuts") * share, share, 0)
    return summed.astype(jnp.bfloat16)


def solution(mesh):
    in_specs = (
        P("cuts", None, "group", None),
        P("cuts", None, None, None),
        P("group", None),
        P("group"),
    )
    out_specs = P("cuts", "group", None)
    return jax.shard_map(local, mesh=mesh, in_specs=in_specs, out_specs=out_specs, check_vma=False)
```

profile of v0, /device:TPU:0, one launch (start us, length us, event | category | flops | bytes accessed | tf_op | source)
XLA Modules:
  0.0 309.5 jit_solution(17406738748968861879)
XLA Ops:
  6.5 0.0 copy-start.1
  6.5 0.0 copy-start
  6.5 0.0 copy-start.2
  6.5 7.5 %all-to-all-start = ((bf16[64,64,512]{2,1,0:T(8,128)(2,1)}), bf16[64,64,512]{2,1,0:T(8,128)(2,1)}, u32[]{:S(2)}, u32[]{:S(2)}) async-start(bf16[64,64,512]{2,1,0:T(8,128)(2,1)} %bitcast.29), calls=%async_computation | async-start | bytes 8388608 | tf_op jit(solution)/shard_map/all_to_all | solution.py:16
  14.1 0.0 all-reduce.2.cloned.1.call-start
  14.1 0.0 copy-done.1
  14.2 0.0 copy-done
  14.2 0.1 copy.9
  14.3 0.1 copy.10
  14.4 0.0 copy-done.2
  14.4 0.1 iota_compare_fusion
  14.6 77.2 %all-to-all-done = bf16[64,64,512]{2,1,0:T(8,128)(2,1)} async-done(((bf16[64,64,512]{2,1,0:T(8,128)(2,1)}), bf16[64,64,512]{2,1,0:T(8,128)(2,1)}, u32[]{:S(2)}, u32[]{:S(2)}) %all-to-all-start) | async-done | bytes 4194336 | tf_op jit(solution)/shard_map/all_to_all | solution.py:16
  91.8 4.6 %copy.7 = bf16[16,4,64,512]{3,2,0,1:T(8,128)(2,1)} copy(bf16[16,4,64,512]{3,2,1,0:T(8,128)(2,1)} %bitcast.4) | data formatting | bytes 8388608 | tf_op jit(solution)/shard_map/all_to_all | solution.py:16
  96.4 72.6 %gather_fusion = bf16[4096,512]{1,0:T(8,128)(2,1)} fusion(bf16[4,1024,512]{2,1,0:T(8,128)(2,1)} %bitcast.26, s32[4096]{0:T(1024)S(1)} %bitcast.27), kind=kCustom, calls=%fused_computation | custom fusion | bytes 8421376 | tf_op jit(solution)/shard_map/jit(take_along_axis)/gather | solution.py:22
  169.0 5.8 %fusion = bf16[1024,4,512]{0,2,1:T(8,128)(2,1)} fusion(pred[1024,4]{0,1:T(4,128)(4,1)S(1)} %iota_compare_fusion, bf16[4,1024,512]{2,1,0:T(8,128)(2,1)} %bitcast.28, pred[4,1024]{1,0:T(4,128)(4,1)S(1)} %compare_and_fusion, bf16[256,256]{0,1:T(8,128)(2,1)S(1)} %bitcast.31, bf16[256,256]{0,1:T(8,128)(2,1)S(1)} %bitcast_negate_fusion, ...), kind=kOutput, calls=%fused_computation.2 | convolution fusion | flops 2155872256 | bytes 8790016 | tf_op jit(solution)/shard_map/gcr,rs->cgs/dot_general | solution.py:23
  174.8 0.0 all-reduce.2.cloned.1.call-update
  174.9 123.0 %all-reduce.2.cloned.1.call-done = bf16[1024,4,512]{0,2,1:T(8,128)(2,1)} async-done(((bf16[1024,4,512]{0,2,1:T(8,128)(2,1)}), bf16[1024,4,512]{0,2,1:T(8,128)(2,1)}) %all-reduce.2.cloned.1.call-update) | async-done | bytes 4194320 | tf_op jit(solution)/shard_map/psum | solution.py:24
  297.9 1.7 convert_convert_fusion
  299.6 3.1 copy.8
  (5 shorter events, 0.1 us)
Async XLA Ops:
  6.5 7.6 %copy-start.1 = (s32[4,1024]{1,0:T(4,128)S(1)}, s32[4,1024]{1,0:T(4,128)}, u32[]{:S(2)}) copy-start(s32[4,1024]{1,0:T(4,128)} %param.6) | copy-start | bytes 49156
  6.5 7.6 %copy-start = (bf16[1,2,256,256]{3,2,1,0:T(8,128)(2,1)S(1)}, bf16[1,2,256,256]{3,2,1,0:T(8,128)(2,1)}, u32[]{:S(2)}) copy-start(bf16[1,2,256,256]{3,2,1,0:T(8,128)(2,1)} %param.5) | copy-start | bytes 786436
  6.5 7.9 %copy-start.2 = (s32[4]{0:T(128)S(1)}, s32[4]{0:T(128)}, u32[]{:S(2)}) copy-start(s32[4]{0:T(128)} %param.7) | copy-start | bytes 52
  6.5 85.2 %all-to-all-start = ((bf16[64,64,512]{2,1,0:T(8,128)(2,1)}), bf16[64,64,512]{2,1,0:T(8,128)(2,1)}, u32[]{:S(2)}, u32[]{:S(2)}) async-start(bf16[64,64,512]{2,1,0:T(8,128)(2,1)} %bitcast.29), calls=%async_computation | async-start | bytes 8388608 | tf_op jit(solution)/shard_map/all_to_all | solution.py:16
  14.1 283.8 %all-reduce.2.cloned.1.call-start = ((), (), s32[]{:S(2)}) async-start(), calls=%async_computation.1 | async-start | bytes 8388608 | tf_op jit(solution)/shard_map/psum | solution.py:24
Sparse Core Ops, SparseCore 0:
  175.0 122.8 all-reduce.1
where the time goes:
time: 311 us; the launch traced here: 310 us
  waiting for transfers between devices  200 us (64%)
  local copies, waits for them, and re-layouts  80.5 us (26%)
  between operations  13.5 us (4%)
  starting transfers between devices  7.58 us (2%)
  matrix products  5.84 us (2%)
    psum x1, waiting for transfers between devices, local(): lax.psum(jnp.where(jnp.transpose(live_mask)[:, :, None], product, jnp.flo...  123 us
    all_to_all x1, waiting for transfers between devices, local(): lax.all_to_all(stem_blocks[0], 'group', split_axis=0, concat_axis=1, tile...  77.2 us
    gather x1, local copies, waits for them, and re-layouts, local(): picked = jnp.take_along_axis(owned_rows, slot_rows[:, :, None], axis=1)  72.6 us
    all_to_all x1, starting transfers between devices, local(): lax.all_to_all(stem_blocks[0], 'group', split_axis=0, concat_axis=1, tile...  7.54 us
  transfers between devices with their start and end apart: 2, of which 2 were waited for; matrix products, arithmetic and copies ran while one was open for 0% of the time, Pallas kernels for 0%

commit v1 on v0

--- a/solution.py
+++ b/solution.py
@@ -13,7 +13,15 @@
 
 
 def local(stem_blocks, cap_tensor, slot_rows, counts):
-    owned_rows = lax.all_to_all(stem_blocks[0], "group", split_axis=0, concat_axis=1, tiled=True)
+    ways, here = (lax.axis_size("group"), lax.axis_index("group"))
+    width = stem_blocks[0].shape[0] // ways
+    turned = jnp.roll(stem_blocks[0], -here * width, axis=0)
+    got = [lax.slice_in_dim(turned, 0, width, axis=0)]
+    for far in range(1, ways):
+        sent = lax.slice_in_dim(turned, far * width, (far + 1) * width, axis=0)
+        got.append(lax.ppermute(sent, "group", [(d, (d + far) % ways) for d in range(ways)]))
+    line = jnp.concatenate(got[::-1], axis=1)
+    owned_rows = jnp.roll(line, (here + 1) * got[0].shape[1], axis=1)
     matrix = build_matrix(cap_tensor[0])
     slot_total = slot_rows.shape[1]
     share = slot_total // lax.axis_size("cuts")

time: 311 us -> 320 us (1.029)
  waiting for transfers between devices: 200 us -> 168 us
  starting transfers between devices: 7.58 us -> 39.2 us
  other arithmetic: 1.84 us -> 7.48 us
  local copies, waits for them, and re-layouts: 80.5 us -> 85 us
    all_to_all x1 -> x0, waiting for transfers between devices: 77.2 us -> none  [local(): lax.all_to_all(stem_blocks[0], 'group', split_axis=0, concat_axis=1, tile...]
    ppermute x0 -> x15, waiting for transfers between devices: none -> 61.4 us  [local(): lax.ppermute(sent, 'group', [(d, (d + far) % ways) for d in range(ways)])]
    ppermute x0 -> x15, starting transfers between devices: none -> 39.2 us  [local(): lax.ppermute(sent, 'group', [(d, (d + far) % ways) for d in range(ways)])]
    psum x1, waiting for transfers between devices: 123 us -> 107 us  [local(): lax.psum(jnp.where(jnp.transpose(live_mask)[:, :, None], product, jnp.flo...]
    all_to_all x1 -> x0, starting transfers between devices: 7.54 us -> none  [local(): lax.all_to_all(stem_blocks[0], 'group', split_axis=0, concat_axis=1, tile...]
    unnamed x9 -> x46, local copies, waits for them, and re-layouts: 0.21 us -> 5.04 us
    all_to_all x1 -> x0, local copies, waits for them, and re-layouts: 4.63 us -> none  [local(): lax.all_to_all(stem_blocks[0], 'group', split_axis=0, concat_axis=1, tile...]
    concatenate x0 -> x1, other arithmetic: none -> 3.2 us  [local(): turned = jnp.roll(stem_blocks[0], -here * width, axis=0)]
  transfers between devices with their start and end apart: 2 -> 16, of which waited for: 2 -> 11; matrix products, arithmetic and copies ran while one was open for 0% -> 1% of each run, Pallas kernels for 0% -> 0%
where the time goes in v1:
time: 320 us; the launch traced here: 319 us
  waiting for transfers between devices  168 us (52%)
  local copies, waits for them, and re-layouts  85 us (27%)
  starting transfers between devices  39.2 us (12%)
  between operations  13.7 us (4%)
  other arithmetic  7.48 us (2%)
  matrix products  5.86 us (2%)
    psum x1, waiting for transfers between devices, local(): lax.psum(jnp.where(jnp.transpose(live_mask)[:, :, None], product, jnp.flo...  107 us
    gather x1, local copies, waits for them, and re-layouts, local(): picked = jnp.take_along_axis(owned_rows, slot_rows[:, :, None], axis=1)  72.3 us
    ppermute x15, waiting for transfers between devices, local(): lax.ppermute(sent, 'group', [(d, (d + far) % ways) for d in range(ways)])  61.4 us
    ppermute x15, starting transfers between devices, local(): lax.ppermute(sent, 'group', [(d, (d + far) % ways) for d in range(ways)])  39.2 us
  transfers between devices with their start and end apart: 16, of which 11 were waited for; matrix products, arithmetic and copies ran while one was open for 1% of the time, Pallas kernels for 0%

profile of v1, /device:TPU:0, one launch (start us, length us, event | category | flops | bytes accessed | tf_op | source)
XLA Modules:
  0.0 319.4 jit_solution(5867851448538572269)
XLA Ops:
  6.5 3.2 %fusion.1 = bf16[64,64,512]{2,1,0:T(8,128)(2,1)S(1)} fusion(s32[]{:T(128)S(6)} %select_n.43, bf16[64,64,512]{2,1,0:T(8,128)(2,1)} %bitcast.24), kind=kLoop, calls=%fused_computation.5 | loop fusion | flops 2097152 | bytes 8388612 | tf_op jit(solution)/shard_map/jit(_roll_dynamic)/concatenate | solution.py:18
  9.8 1.9 copy-done
  11.7 1.3 fusion.17
  13.0 5.4 %collective-permute-start = (bf16[4,64,512]{2,1,0:T(8,128)(2,1)}, bf16[4,64,512]{2,1,0:T(8,128)(2,1)S(1)}, u32[]{:S(2)}, u32[]{:S(2)}) collective-permute-start(bf16[4,64,512]{2,1,0:T(8,128)(2,1)} %get-tuple-element.19), channel_id=1, source_target_pairs={{0,15},{1,0},{2,1},{3,2},{4,3},{5,4},{6,5},{7,6},{8,7},{9,8},{10,9... | collective-permute-start | bytes 786440 | tf_op jit(solution)/shard_map/ppermute | solution.py:22
  21.2 1.3 iota_compare_fusion
  23.9 1.5 collective-permute-done
  25.4 2.9 collective-permute-start.5
  28.3 2.7 collective-permute-done.1
  31.0 5.6 %collective-permute-done.2 = bf16[4,64,512]{2,1,0:T(8,128)(2,1)S(1)} collective-permute-done((bf16[4,64,512]{2,1,0:T(8,128)(2,1)}, bf16[4,64,512]{2,1,0:T(8,128)(2,1)S(1)}, u32[]{:S(2)}, u32[]{:S(2)}) %collective-permute-start.2) | collective-permute-done | bytes 262176 | tf_op jit(solution)/shard_map/ppermute | solution.py:22
  36.7 5.6 %collective-permute-done.3 = bf16[4,64,512]{2,1,0:T(8,128)(2,1)S(1)} collective-permute-done((bf16[4,64,512]{2,1,0:T(8,128)(2,1)}, bf16[4,64,512]{2,1,0:T(8,128)(2,1)S(1)}, u32[]{:S(2)}, u32[]{:S(2)}) %collective-permute-start.3) | collective-permute-done | bytes 262176 | tf_op jit(solution)/shard_map/ppermute | solution.py:22
  42.3 5.6 %collective-permute-done.4 = bf16[4,64,512]{2,1,0:T(8,128)(2,1)S(1)} collective-permute-done((bf16[4,64,512]{2,1,0:T(8,128)(2,1)}, bf16[4,64,512]{2,1,0:T(8,128)(2,1)S(1)}, u32[]{:S(2)}, u32[]{:S(2)}) %collective-permute-start.4) | collective-permute-done | bytes 262176 | tf_op jit(solution)/shard_map/ppermute | solution.py:22
  47.9 5.6 %collective-permute-done.5 = bf16[4,64,512]{2,1,0:T(8,128)(2,1)S(1)} collective-permute-done((bf16[4,64,512]{2,1,0:T(8,128)(2,1)}, bf16[4,64,512]{2,1,0:T(8,128)(2,1)S(1)}, u32[]{:S(2)}, u32[]{:S(2)}) %collective-permute-start.5) | collective-permute-done | bytes 262176 | tf_op jit(solution)/shard_map/ppermute | solution.py:22
  53.5 18.2 %collective-permute-start.10 = (bf16[4,64,512]{2,1,0:T(8,128)(2,1)S(1)}, bf16[4,64,512]{2,1,0:T(8,128)(2,1)S(1)}, u32[]{:S(2)}, u32[]{:S(2)}) collective-permute-start(bf16[4,64,512]{2,1,0:T(8,128)(2,1)S(1)} %get-tuple-element.9), channel_id=1, source_target_pairs={{0,5},{1,6},{2,7},{3,8},{4,9},{5,10},{6,11},{7,12},{8,13},{9,14},{... | collective-permute-start | bytes 786440 | tf_op jit(solution)/shard_map/ppermute | solution.py:22
  71.7 11.3 %collective-permute-start.11 = (bf16[4,64,512]{2,1,0:T(8,128)(2,1)S(1)}, bf16[4,64,512]{2,1,0:T(8,128)(2,1)S(1)}, u32[]{:S(2)}, u32[]{:S(2)}) collective-permute-start(bf16[4,64,512]{2,1,0:T(8,128)(2,1)S(1)} %get-tuple-element.8), channel_id=1, source_target_pairs={{0,4},{1,5},{2,6},{3,7},{4,8},{5,9},{6,10},{7,11},{8,12},{9,13},{1... | collective-permute-start | bytes 786440 | tf_op jit(solution)/shard_map/ppermute | solution.py:22
  83.0 23.5 %collective-permute-done.7 = bf16[4,64,512]{2,1,0:T(8,128)(2,1)S(1)} collective-permute-done((bf16[4,64,512]{2,1,0:T(8,128)(2,1)}, bf16[4,64,512]{2,1,0:T(8,128)(2,1)S(1)}, u32[]{:S(2)}, u32[]{:S(2)}) %collective-permute-start.7) | collective-permute-done | bytes 262176 | tf_op jit(solution)/shard_map/ppermute | solution.py:22
  106.9 7.3 %collective-permute-done.12 = bf16[4,64,512]{2,1,0:T(8,128)(2,1)S(1)} collective-permute-done((bf16[4,64,512]{2,1,0:T(8,128)(2,1)S(1)}, bf16[4,64,512]{2,1,0:T(8,128)(2,1)S(1)}, u32[]{:S(2)}, u32[]{:S(2)}) %collective-permute-start.12) | collective-permute-done | bytes 262176 | tf_op jit(solution)/shard_map/ppermute | solution.py:22
  114.2 3.9 %collective-permute-done.13 = bf16[4,64,512]{2,1,0:T(8,128)(2,1)S(1)} collective-permute-done((bf16[4,64,512]{2,1,0:T(8,128)(2,1)S(1)}, bf16[4,64,512]{2,1,0:T(8,128)(2,1)S(1)}, u32[]{:S(2)}, u32[]{:S(2)}) %collective-permute-start.13) | collective-permute-done | bytes 262176 | tf_op jit(solution)/shard_map/ppermute | solution.py:22
  118.1 1.0 slice_dynamic-update-slice_fusion
  120.5 2.3 constant_dynamic-slice_fusion
  122.8 72.3 %gather_fusion = bf16[4096,512]{1,0:T(8,128)(2,1)} fusion(bf16[4,1024,512]{2,1,0:T(8,128)(2,1)} %constant_dynamic-slice_fusion, s32[4096]{0:T(1024)S(1)} %bitcast.22), kind=kCustom, calls=%fused_computation | custom fusion | bytes 8421376 | tf_op jit(solution)/shard_map/jit(take_along_axis)/gather | solution.py:30
  195.1 5.9 %fusion = bf16[1024,4,512]{0,2,1:T(8,128)(2,1)} fusion(pred[1024,4]{0,1:T(4,128)(4,1)S(1)} %copy-done.5, bf16[4,1024,512]{2,1,0:T(8,128)(2,1)} %bitcast.23, pred[4,1024]{1,0:T(4,128)(4,1)S(1)} %copy-done.4, bf16[256,256]{0,1:T(8,128)(2,1)S(1)} %bitcast.26, bf16[256,256]{0,1:T(8,128)(2,1)S(1)} %bitcast_negate_fusion, bf16[256,256]{0,1:T(8,128)(2,1)S(1)} %bitcast.25), kind=kOutput, calls=%fused_computation.4 | convolution fusion | flops 2155872256 | bytes 8790016 | tf_op jit(solution)/shard_map/gcr,rs->cgs/dot_general | solution.py:31
  201.0 106.7 %all-reduce.2.cloned.1.call-done = bf16[1024,4,512]{0,2,1:T(8,128)(2,1)} async-done(((bf16[1024,4,512]{0,2,1:T(8,128)(2,1)}), bf16[1024,4,512]{0,2,1:T(8,128)(2,1)}) %all-reduce.2.cloned.1.call-update) | async-done | bytes 4194320 | tf_op jit(solution)/shard_map/psum | solution.py:32
  307.7 1.7 convert_convert_fusion
  309.5 3.1 copy.7
  (68 shorter events, 5.9 us)
Async XLA Ops:
  6.5 13.3 %copy-start.3 = (s32[4,1024]{1,0:T(4,128)S(1)}, s32[4,1024]{1,0:T(4,128)}, u32[]{:S(2)}) copy-start(s32[4,1024]{1,0:T(4,128)} %param.6) | copy-start | bytes 49156
  6.5 301.2 %all-reduce.2.cloned.1.call-start = ((), (), s32[]{:S(2)}) async-start(), calls=%async_computation | async-start | bytes 8388608 | tf_op jit(solution)/shard_map/psum | solution.py:32
  6.5 13.9 %copy-start.1 = (bf16[1,2,256,256]{3,2,1,0:T(8,128)(2,1)S(1)}, bf16[1,2,256,256]{3,2,1,0:T(8,128)(2,1)}, u32[]{:S(2)}) copy-start(bf16[1,2,256,256]{3,2,1,0:T(8,128)(2,1)} %param.5) | copy-start | bytes 786436
  9.8 1.9 copy-start
  13.0 12.4 %collective-permute-start = (bf16[4,64,512]{2,1,0:T(8,128)(2,1)}, bf16[4,64,512]{2,1,0:T(8,128)(2,1)S(1)}, u32[]{:S(2)}, u32[]{:S(2)}) collective-permute-start(bf16[4,64,512]{2,1,0:T(8,128)(2,1)} %get-tuple-element.19), channel_id=1, source_target_pairs={{0,15},{1,0},{2,1},{3,2},{4,3},{5,4},{6,5},{7,6},{8,7},{9,8},{10,9... | collective-permute-start | bytes 786440 | tf_op jit(solution)/shard_map/ppermute | solution.py:22
  18.4 12.6 %collective-permute-start.1 = (bf16[4,64,512]{2,1,0:T(8,128)(2,1)}, bf16[4,64,512]{2,1,0:T(8,128)(2,1)S(1)}, u32[]{:S(2)}, u32[]{:S(2)}) collective-permute-start(bf16[4,64,512]{2,1,0:T(8,128)(2,1)} %get-tuple-element.18), channel_id=1, source_target_pairs={{0,14},{1,15},{2,0},{3,1},{4,2},{5,3},{6,4},{7,5},{8,6},{9,7},{10,... | collective-permute-start | bytes 786440 | tf_op jit(solution)/shard_map/ppermute | solution.py:22
  19.0 17.7 %collective-permute-start.2 = (bf16[4,64,512]{2,1,0:T(8,128)(2,1)}, bf16[4,64,512]{2,1,0:T(8,128)(2,1)S(1)}, u32[]{:S(2)}, u32[]{:S(2)}) collective-permute-start(bf16[4,64,512]{2,1,0:T(8,128)(2,1)} %get-tuple-element.17), channel_id=1, source_target_pairs={{0,13},{1,14},{2,15},{3,0},{4,1},{5,2},{6,3},{7,4},{8,5},{9,6},{10... | collective-permute-start | bytes 786440 | tf_op jit(solution)/shard_map/ppermute | solution.py:22
  19.2 23.1 %collective-permute-start.3 = (bf16[4,64,512]{2,1,0:T(8,128)(2,1)}, bf16[4,64,512]{2,1,0:T(8,128)(2,1)S(1)}, u32[]{:S(2)}, u32[]{:S(2)}) collective-permute-start(bf16[4,64,512]{2,1,0:T(8,128)(2,1)} %get-tuple-element.16), channel_id=1, source_target_pairs={{0,12},{1,13},{2,14},{3,15},{4,0},{5,1},{6,2},{7,3},{8,4},{9,5},{1... | collective-permute-start | bytes 786440 | tf_op jit(solution)/shard_map/ppermute | solution.py:22
  19.7 28.1 %collective-permute-start.4 = (bf16[4,64,512]{2,1,0:T(8,128)(2,1)}, bf16[4,64,512]{2,1,0:T(8,128)(2,1)S(1)}, u32[]{:S(2)}, u32[]{:S(2)}) collective-permute-start(bf16[4,64,512]{2,1,0:T(8,128)(2,1)} %get-tuple-element.15), channel_id=1, source_target_pairs={{0,11},{1,12},{2,13},{3,14},{4,15},{5,0},{6,1},{7,2},{8,3},{9,4},{... | collective-permute-start | bytes 786440 | tf_op jit(solution)/shard_map/ppermute | solution.py:22
  25.4 28.1 %collective-permute-start.5 = (bf16[4,64,512]{2,1,0:T(8,128)(2,1)}, bf16[4,64,512]{2,1,0:T(8,128)(2,1)S(1)}, u32[]{:S(2)}, u32[]{:S(2)}) collective-permute-start(bf16[4,64,512]{2,1,0:T(8,128)(2,1)} %get-tuple-element.14), channel_id=1, source_target_pairs={{0,10},{1,11},{2,12},{3,13},{4,14},{5,15},{6,0},{7,1},{8,2},{9,3},... | collective-permute-start | bytes 786440 | tf_op jit(solution)/shard_map/ppermute | solution.py:22
  31.0 40.7 %collective-permute-start.6 = (bf16[4,64,512]{2,1,0:T(8,128)(2,1)}, bf16[4,64,512]{2,1,0:T(8,128)(2,1)S(1)}, u32[]{:S(2)}, u32[]{:S(2)}) collective-permute-start(bf16[4,64,512]{2,1,0:T(8,128)(2,1)} %get-tuple-element.13), channel_id=1, source_target_pairs={{0,9},{1,10},{2,11},{3,12},{4,13},{5,14},{6,15},{7,0},{8,1},{9,2},... | collective-permute-start | bytes 786440 | tf_op jit(solution)/shard_map/ppermute | solution.py:22
  36.6 70.0 %collective-permute-start.7 = (bf16[4,64,512]{2,1,0:T(8,128)(2,1)}, bf16[4,64,512]{2,1,0:T(8,128)(2,1)S(1)}, u32[]{:S(2)}, u32[]{:S(2)}) collective-permute-start(bf16[4,64,512]{2,1,0:T(8,128)(2,1)} %get-tuple-element.12), channel_id=1, source_target_pairs={{0,8},{1,9},{2,10},{3,11},{4,12},{5,13},{6,14},{7,15},{8,0},{9,1},... | collective-permute-start | bytes 786440 | tf_op jit(solution)/shard_map/ppermute | solution.py:22
  42.3 64.4 %collective-permute-start.8 = (bf16[4,64,512]{2,1,0:T(8,128)(2,1)S(1)}, bf16[4,64,512]{2,1,0:T(8,128)(2,1)S(1)}, u32[]{:S(2)}, u32[]{:S(2)}) collective-permute-start(bf16[4,64,512]{2,1,0:T(8,128)(2,1)S(1)} %get-tuple-element.11), channel_id=1, source_target_pairs={{0,7},{1,8},{2,9},{3,10},{4,11},{5,12},{6,13},{7,14},{8,15},{9,0},... | collective-permute-start | bytes 786440 | tf_op jit(solution)/shard_map/ppermute | solution.py:22
  47.9 58.9 %collective-permute-start.9 = (bf16[4,64,512]{2,1,0:T(8,128)(2,1)S(1)}, bf16[4,64,512]{2,1,0:T(8,128)(2,1)S(1)}, u32[]{:S(2)}, u32[]{:S(2)}) collective-permute-start(bf16[4,64,512]{2,1,0:T(8,128)(2,1)S(1)} %get-tuple-element.10), channel_id=1, source_target_pairs={{0,6},{1,7},{2,8},{3,9},{4,10},{5,11},{6,12},{7,13},{8,14},{9,15},... | collective-permute-start | bytes 786440 | tf_op jit(solution)/shard_map/ppermute | solution.py:22
  53.5 53.3 %collective-permute-start.10 = (bf16[4,64,512]{2,1,0:T(8,128)(2,1)S(1)}, bf16[4,64,512]{2,1,0:T(8,128)(2,1)S(1)}, u32[]{:S(2)}, u32[]{:S(2)}) collective-permute-start(bf16[4,64,512]{2,1,0:T(8,128)(2,1)S(1)} %get-tuple-element.9), channel_id=1, source_target_pairs={{0,5},{1,6},{2,7},{3,8},{4,9},{5,10},{6,11},{7,12},{8,13},{9,14},{... | collective-permute-start | bytes 786440 | tf_op jit(solution)/shard_map/ppermute | solution.py:22
  71.7 35.2 %collective-permute-start.11 = (bf16[4,64,512]{2,1,0:T(8,128)(2,1)S(1)}, bf16[4,64,512]{2,1,0:T(8,128)(2,1)S(1)}, u32[]{:S(2)}, u32[]{:S(2)}) collective-permute-start(bf16[4,64,512]{2,1,0:T(8,128)(2,1)S(1)} %get-tuple-element.8), channel_id=1, source_target_pairs={{0,4},{1,5},{2,6},{3,7},{4,8},{5,9},{6,10},{7,11},{8,12},{9,13},{1... | collective-permute-start | bytes 786440 | tf_op jit(solution)/shard_map/ppermute | solution.py:22
  106.6 7.6 %collective-permute-start.12 = (bf16[4,64,512]{2,1,0:T(8,128)(2,1)S(1)}, bf16[4,64,512]{2,1,0:T(8,128)(2,1)S(1)}, u32[]{:S(2)}, u32[]{:S(2)}) collective-permute-start(bf16[4,64,512]{2,1,0:T(8,128)(2,1)S(1)} %get-tuple-element.7), channel_id=1, source_target_pairs={{0,3},{1,4},{2,5},{3,6},{4,7},{5,8},{6,9},{7,10},{8,11},{9,12},{10... | collective-permute-start | bytes 786440 | tf_op jit(solution)/shard_map/ppermute | solution.py:22
  106.7 11.4 %collective-permute-start.13 = (bf16[4,64,512]{2,1,0:T(8,128)(2,1)S(1)}, bf16[4,64,512]{2,1,0:T(8,128)(2,1)S(1)}, u32[]{:S(2)}, u32[]{:S(2)}) collective-permute-start(bf16[4,64,512]{2,1,0:T(8,128)(2,1)S(1)} %get-tuple-element.6), channel_id=1, source_target_pairs={{0,2},{1,3},{2,4},{3,5},{4,6},{5,7},{6,8},{7,9},{8,10},{9,11},{10,... | collective-permute-start | bytes 786440 | tf_op jit(solution)/shard_map/ppermute | solution.py:22
  106.7 11.4 %collective-permute-start.14 = (bf16[4,64,512]{2,1,0:T(8,128)(2,1)S(1)}, bf16[4,64,512]{2,1,0:T(8,128)(2,1)S(1)}, u32[]{:S(2)}, u32[]{:S(2)}) collective-permute-start(bf16[4,64,512]{2,1,0:T(8,128)(2,1)S(1)} %get-tuple-element.5), channel_id=1, source_target_pairs={{0,1},{1,2},{2,3},{3,4},{4,5},{5,6},{6,7},{7,8},{8,9},{9,10},{10,1... | collective-permute-start | bytes 786440 | tf_op jit(solution)/shard_map/ppermute | solution.py:22
  122.8 72.3 %copy-start.2 = (bf16[1,1,256,256]{2,3,1,0:T(8,128)(2,1)S(1)}, bf16[1,1,256,256]{2,3,1,0:T(8,128)(2,1)}, u32[]{:S(2)}) copy-start(bf16[1,1,256,256]{2,3,1,0:T(8,128)(2,1)} %copy.8) | copy-start | bytes 393220
  122.8 72.3 %copy-start.4 = (pred[4,1024]{1,0:T(4,128)(4,1)S(1)}, pred[4,1024]{1,0:T(4,128)(4,1)}, u32[]{:S(2)}) copy-start(pred[4,1024]{1,0:T(4,128)(4,1)} %compare_and_fusion) | copy-start | bytes 12292
  122.8 72.3 %copy-start.5 = (pred[1024,4]{0,1:T(4,128)(4,1)S(1)}, pred[1024,4]{0,1:T(4,128)(4,1)}, u32[]{:S(2)}) copy-start(pred[1024,4]{0,1:T(4,128)(4,1)} %iota_compare_fusion) | copy-start | bytes 12292
Sparse Core Ops, SparseCore 0:
  201.1 106.5 all-reduce.1
